TPU v7x, 32 devices: a whole 2x2x4 slice. The times are simulated.
32 devices in a mesh: segment: 4 (over y, core), chan: 4 (over z), tm: 2 (over x).
Axes of the slice: x: 2, y: 2, z: 4, core: 2. Of those that a mesh axis runs over, the one named last changes fastest.
Arguments:
- voltages: bfloat16 [3, 512, 2048, 128], P(None, 'chan', ('segment', 'tm')), may hold values from -6 to 6
- flags: int32 [512], P('chan'), may hold values 0 or 1
- delays: int32 [512, 512], replicated, may hold values from 0 to 127
- analysis_taps: float32 [4, 64], replicated, may hold values from -3 to 3
- synthesis_taps: float32 [4, 64], replicated, may hold values from -3 to 3
Outputs:
- vis: float32 [64, 8, 2, 512, 512], P('chan', ('segment', 'tm'))
- beams: bfloat16 [3, 512, 2048, 128], P(None, 'chan', ('segment', 'tm'))
All inputs are finite; a program needn't handle non-finite values. No bound on the sum of `flags` on one device may be relied on, other than what follows from the above.
Results may differ from a plain program's by a relative error of at most 0.008.
Values may be sent and summed in bfloat16 or wider, within the bound.
A program may use at most 256 MiB of HBM per device.

v0:
```python
import math
import jax
import jax.numpy as jnp
from jax import lax
from jax.sharding import PartitionSpec as P

A = 512
C = 64
TAPS = 4
FB = 256
MB = 3


def shifted(value, axis, steps):
    count = lax.axis_size(axis)
    leading, last = (max(0, -steps), min(count, count - steps))
    return lax.ppermute(value, axis, [(source, source + steps) for source in range(leading, last)])


def forward_table(chan_count):
    indices = jnp.arange(2 * chan_count, dtype=jnp.int32)
    out_chan = indices // 2
    out_part = indices % 2
    in_part = indices // chan_count
    in_sample = indices % chan_count
    wrapped = out_chan[:, None] * in_sample[None, :] % chan_count
    angles = wrapped.astype(jnp.float32) * (2.0 * math.pi / chan_count)
    cosine = jnp.cos(angles)
    sine_part = jnp.sin(angles)
    real_row = jnp.where(in_part[None, :] == 0, cosine, sine_part)
    imag_row = jnp.where(in_part[None, :] == 0, -sine_part, cosine)
    dft_table = jnp.where(out_part[:, None] == 0, real_row, imag_row)
    return (dft_table * (1.0 / math.sqrt(chan_count))).astype(jnp.bfloat16)


def inverse_table(chan_count):
    indices = jnp.arange(2 * chan_count, dtype=jnp.int32)
    out_part = indices // chan_count
    out_sample = indices % chan_count
    in_chan = indices // 2
    in_part = indices % 2
    wrapped = out_sample[:, None] * in_chan[None, :] % chan_count
    angles = wrapped.astype(jnp.float32) * (2.0 * math.pi / chan_count)
    cosine = jnp.cos(angles)
    sine_part = jnp.sin(angles)
    real_row = jnp.where(in_part[None, :] == 0, cosine, -sine_part)
    imag_row = jnp.where(in_part[None, :] == 0, sine_part, cosine)
    dft_table = jnp.where(out_part[:, None] == 0, real_row, imag_row)
    return (dft_table * (1.0 / math.sqrt(chan_count))).astype(jnp.bfloat16)


def steering_weights(delays, channel_list, chan_count):
    odd_steps = 2 * channel_list + 1
    wrapped = odd_steps[:, None, None] * delays[None, :, :] % (2 * chan_count)
    angles = wrapped.astype(jnp.float32) * (math.pi / chan_count)
    cosine = jnp.swapaxes(jnp.cos(angles), 1, 2)
    sine_part = jnp.swapaxes(jnp.sin(angles), 1, 2)
    upper = jnp.concatenate([cosine, sine_part], axis=2)
    lower = jnp.concatenate([-sine_part, cosine], axis=2)
    return jnp.concatenate([upper, lower], axis=1).astype(jnp.bfloat16)


def channelize(block, rim, paired_filter_taps, forward, flag_scale):
    history = paired_filter_taps.shape[0] - 1
    frames = block.shape[1]
    padded = jnp.concatenate([rim.astype(jnp.float32), block.astype(jnp.float32)], axis=1)
    weighted = paired_filter_taps[0] * padded[:, history : history + frames]
    for tap_number in range(1, history + 1):
        weighted = (
            weighted
            + paired_filter_taps[tap_number]
            * padded[:, history - tap_number : history - tap_number + frames]
        )
    weighted = weighted.astype(jnp.bfloat16)
    spectra = jnp.einsum("oi,afi->oaf", forward, weighted, preferred_element_type=jnp.float32)
    spectra = spectra * flag_scale[None, :, None]
    return spectra.astype(jnp.bfloat16).reshape(forward.shape[0] // 2, 2, block.shape[0], frames)


def gram_block(turned):
    left_part = jnp.concatenate([turned[:, 0], turned[:, 1]], axis=-1)
    rotated = jnp.concatenate([turned[:, 1], -turned[:, 0]], axis=-1)
    stacked = jnp.concatenate([left_part, rotated], axis=1)
    return jnp.einsum("cif,cjf->cij", stacked, left_part, preferred_element_type=jnp.float32)


def form_beams(turned, steering_matrix):
    chan_local, parts, antennas, frames = turned.shape
    flattened_rows = turned.reshape(chan_local, parts * antennas, frames)
    formed_beams = jnp.einsum(
        "goq,gqk->gok", steering_matrix, flattened_rows, preferred_element_type=jnp.float32
    )
    formed_beams = (formed_beams * (1.0 / math.sqrt(antennas))).astype(jnp.bfloat16)
    return formed_beams.reshape(chan_local, 2, steering_matrix.shape[1] // 2, frames)


def tail_frames(inverse_part, count, history):
    beam_local, frames, width_both = inverse_part.shape
    block_frames = frames // count
    blocks = inverse_part.reshape(beam_local, count, block_frames, width_both)
    return blocks[:, :, block_frames - history :, :]


def synthesize(inverse_part, tails, count, paired_filter_taps):
    history = paired_filter_taps.shape[0] - 1
    beam_local, frames, width_both = inverse_part.shape
    block_frames = frames // count
    blocks = inverse_part.reshape(beam_local, count, block_frames, width_both)
    padded = jnp.concatenate([tails.astype(jnp.float32), blocks.astype(jnp.float32)], axis=2)
    weighted = paired_filter_taps[0] * padded[:, :, history : history + block_frames]
    for tap_number in range(1, history + 1):
        weighted = (
            weighted
            + paired_filter_taps[tap_number]
            * padded[:, :, history - tap_number : history - tap_number + block_frames]
        )
    return jnp.transpose(weighted.astype(jnp.bfloat16), (1, 0, 2, 3))


def per_device(voltages, flags, delays, analysis_taps, synthesis_taps):
    chan_local = C // lax.axis_size("chan")
    history = TAPS - 1
    forward = forward_table(C)
    inverse_result = inverse_table(C)
    analysis_both = jnp.concatenate([analysis_taps, analysis_taps], axis=1)
    synthesis_both = jnp.concatenate([synthesis_taps, synthesis_taps], axis=1)
    flag_scale = flags.astype(jnp.float32)
    channel_list = lax.axis_index("chan") * chan_local + jnp.arange(chan_local, dtype=jnp.int32)
    steering_matrix = steering_weights(delays, channel_list, C)
    rims_all = shifted(voltages[:, :, FB - history :, :], ("segment", "tm"), 1)
    rim_list = [rims_all[batch_step] for batch_step in range(MB)]
    spectra_list = [
        channelize(voltages[batch_step], rim_list[batch_step], analysis_both, forward, flag_scale)
        for batch_step in range(MB)
    ]
    gram_total = None
    beam_list = []
    for batch_step in range(MB):
        turned = lax.all_to_all(
            spectra_list[batch_step], "chan", split_axis=0, concat_axis=2, tiled=True
        )
        gram_piece = gram_block(turned)
        gram_total = gram_piece if batch_step == 0 else gram_total + gram_piece
        piece = lax.all_to_all(
            form_beams(turned, steering_matrix), "chan", split_axis=2, concat_axis=0, tiled=True
        )
        chan_all, parts, beam_local, frames = piece.shape
        flattened_rows = piece.reshape(chan_all * parts, beam_local, frames)
        result = jnp.einsum(
            "oi,ibf->bfo", inverse_result, flattened_rows, preferred_element_type=jnp.float32
        )
        inverse_single = result.astype(jnp.bfloat16)
        tails = shifted(tail_frames(inverse_single, 1, history), ("segment", "tm"), 1)
        beam_list.append(synthesize(inverse_single, tails, 1, synthesis_both))
    beams = jnp.concatenate(beam_list, axis=0)
    vis = (gram_total * (1.0 / (MB * FB))).reshape(chan_local, 1, 2, A, A)
    return (vis, beams)


def solution(mesh):
    placed = (P(None, "chan", ("segment", "tm"), None), P("chan"), P(), P(), P())
    return jax.shard_map(
        per_device,
        mesh=mesh,
        in_specs=placed,
        out_specs=(
            P("chan", ("segment", "tm"), None, None, None),
            P(None, "chan", ("segment", "tm"), None),
        ),
        check_vma=False,
    )
```

profile of v0, /device:TPU:0, one launch (start us, length us, event | category | flops | bytes accessed | tf_op | source)
XLA Modules:
  0.0 1388.2 jit_solution(14261170279806623218)
XLA Ops:
  7.0 23.4 %bitcast_convert_fusion = (f32[128,256,128]{2,1,0:T(8,128)}, f32[128,256,128]{2,1,0:T(8,128)}, f32[128,256,128]{2,1,0:T(8,128)}) fusion(bf16[3,128,256,128]{3,2,1,0:T(8,128)(2,1)} %param.5), kind=kLoop, calls=%fused_computation.133 | loop fusion | flops 12582912 | bytes 75497472 | tf_op jit(solution)/shard_map/convert_element_type | solution.py:66
  30.7 32.0 %multiply_convert_fusion.3 = bf16[128,128,256]{2,0,1:T(8,128)(2,1)} fusion(f32[128]{0:T(128)S(1)} %convert_element_type.152, f32[128,3,128]{2,1,0:T(4,128)S(1)} %copy.50, f32[128,256,128]{2,1,0:T(8,128)} %get-tuple-element.10, f32[128]{0:T(128)S(1)} %get-tuple-element.33, f32[128]{0:T(128)S(1)} %get-tuple-element.34, f32[128]{0:T(128)S(1)} %get-tuple-element.35, ...), kind=kOutput, calls=%fused_computation.121 | convolution fusion | flops 1128595456 | bytes 25366272 | tf_op jit(solution)/shard_map/oi,afi->oaf/dot_general | solution.py:75
  89.7 32.3 %multiply_convert_fusion.4 = bf16[128,128,256]{2,0,1:T(8,128)(2,1)} fusion(f32[128]{0:T(128)S(1)} %convert_element_type.152, f32[128,3,128]{2,1,0:T(4,128)S(1)} %copy.47, f32[128,256,128]{2,1,0:T(8,128)} %get-tuple-element.12, f32[128]{0:T(128)S(1)} %get-tuple-element.33, f32[128]{0:T(128)S(1)} %get-tuple-element.34, f32[128]{0:T(128)S(1)} %get-tuple-element.35, ...), kind=kOutput, calls=%fused_computation.122 | convolution fusion | flops 1128595456 | bytes 25366272 | tf_op jit(solution)/shard_map/oi,afi->oaf/dot_general | solution.py:75
  143.3 129.3 %all-to-all-done.2 = bf16[64,2,128,256]{3,1,2,0:T(2,128)(2,1)} async-done(((bf16[64,2,128,256]{3,1,2,0:T(2,128)(2,1)}), bf16[64,2,128,256]{3,1,2,0:T(2,128)(2,1)}, u32[]{:S(2)}, u32[]{:S(2)}) %all-to-all-start.2) | async-done | bytes 8388640 | tf_op jit(solution)/shard_map/all_to_all | solution.py:139
  278.6 31.9 %multiply_convert_fusion.5 = bf16[128,128,256]{2,0,1:T(8,128)(2,1)} fusion(f32[128]{0:T(128)S(1)} %convert_element_type.152, f32[128,3,128]{2,1,0:T(4,128)S(1)} %copy.44, f32[128,256,128]{2,1,0:T(8,128)} %get-tuple-element.11, f32[128]{0:T(128)S(1)} %get-tuple-element.33, f32[128]{0:T(128)S(1)} %get-tuple-element.34, f32[128]{0:T(128)S(1)} %get-tuple-element.35, ...), kind=kOutput, calls=%fused_computation.123 | convolution fusion | flops 1128595456 | bytes 25366272 | tf_op jit(solution)/shard_map/oi,afi->oaf/dot_general | solution.py:75
  331.7 129.2 %all-to-all-done.1 = bf16[64,2,128,256]{3,1,2,0:T(2,128)(2,1)} async-done(((bf16[64,2,128,256]{3,1,2,0:T(2,128)(2,1)}), bf16[64,2,128,256]{3,1,2,0:T(2,128)(2,1)}, u32[]{:S(2)}, u32[]{:S(2)}) %all-to-all-start.1) | async-done | bytes 8388640 | tf_op jit(solution)/shard_map/all_to_all | solution.py:139
  467.0 70.0 %fusion.102 = (bf16[16,512,512]{2,1,0:T(8,128)(2,1)}, bf16[16,512,512]{2,1,0:T(8,128)(2,1)}, bf16[16,512,512]{2,1,0:T(8,128)(2,1)}) fusion(s32[512,512]{1,0:T(8,128)S(1)} %copy.53, s32[16]{0:T(128)S(1)} %multiply_add_fusion), kind=kLoop, calls=%fused_computation.143 | loop fusion | flops 75497472 | bytes 26214464 | tf_op jit(solution)/shard_map/convert.11
  545.5 21.3 %multiply_convert_fusion.1 = bf16[16,1024,256]{2,1,0:T(8,128)(2,1)} fusion(bf16[16,1024,256]{2,1,0:T(8,128)(2,1)} %bitcast.191, bf16[16,512,512]{2,1,0:T(8,128)(2,1)} %get-tuple-element.21, bf16[16,512,512]{2,1,0:T(8,128)(2,1)} %get-tuple-element.20, bf16[16,512,512]{2,1,0:T(8,128)(2,1)} %get-tuple-element.19), kind=kOutput, calls=%fused_computation.117 | convolution fusion | flops 8732540928 | bytes 41943040 | tf_op jit(solution)/shard_map/goq,gqk->gok/dot_general | solution.py:90
  566.8 16.5 %copy.60 = bf16[16,2,512,256]{3,1,0,2:T(2,128)(2,1)} copy(bf16[16,2,512,256]{3,2,1,0:T(8,128)(2,1)} %bitcast.192) | data formatting | bytes 16777216 | tf_op jit(solution)/shard_map/reshape | solution.py:94
  583.3 66.0 %all-to-all-done = bf16[64,2,128,256]{3,1,2,0:T(2,128)(2,1)} async-done(((bf16[64,2,128,256]{3,1,2,0:T(2,128)(2,1)}), bf16[64,2,128,256]{3,1,2,0:T(2,128)(2,1)}, u32[]{:S(2)}, u32[]{:S(2)}) %all-to-all-start) | async-done | bytes 8388640 | tf_op jit(solution)/shard_map/all_to_all | solution.py:139
  663.8 21.3 %multiply_convert_fusion.2 = bf16[16,1024,256]{2,1,0:T(8,128)(2,1)} fusion(bf16[16,1024,256]{2,1,0:T(8,128)(2,1)} %bitcast.194, bf16[16,512,512]{2,1,0:T(8,128)(2,1)} %get-tuple-element.21, bf16[16,512,512]{2,1,0:T(8,128)(2,1)} %get-tuple-element.20, bf16[16,512,512]{2,1,0:T(8,128)(2,1)} %get-tuple-element.19), kind=kOutput, calls=%fused_computation.118 | convolution fusion | flops 8732540928 | bytes 41943040 | tf_op jit(solution)/shard_map/goq,gqk->gok/dot_general | solution.py:90
  685.1 16.4 %copy.55 = bf16[16,2,512,256]{3,1,0,2:T(2,128)(2,1)} copy(bf16[16,2,512,256]{3,2,1,0:T(8,128)(2,1)} %bitcast.193) | data formatting | bytes 16777216 | tf_op jit(solution)/shard_map/reshape | solution.py:94
  701.5 136.4 %all-to-all-done.4 = bf16[16,2,512,256]{3,1,0,2:T(2,128)(2,1)} async-done(((bf16[16,2,512,256]{3,1,0,2:T(2,128)(2,1)}), bf16[16,2,512,256]{3,1,0,2:T(2,128)(2,1)}, u32[]{:S(2)}, u32[]{:S(2)}) %all-to-all-start.4) | async-done | bytes 8388640 | tf_op jit(solution)/shard_map/all_to_all | solution.py:144
  878.4 21.4 %multiply_convert_fusion = bf16[16,1024,256]{2,1,0:T(8,128)(2,1)} fusion(bf16[16,1024,256]{2,1,0:T(8,128)(2,1)} %bitcast.189, bf16[16,512,512]{2,1,0:T(8,128)(2,1)} %get-tuple-element.21, bf16[16,512,512]{2,1,0:T(8,128)(2,1)} %get-tuple-element.20, bf16[16,512,512]{2,1,0:T(8,128)(2,1)} %get-tuple-element.19), kind=kOutput, calls=%fused_computation.116 | convolution fusion | flops 8732540928 | bytes 41943040 | tf_op jit(solution)/shard_map/goq,gqk->gok/dot_general | solution.py:90
  899.8 16.6 %copy.65 = bf16[16,2,512,256]{3,1,0,2:T(2,128)(2,1)} copy(bf16[16,2,512,256]{3,2,1,0:T(8,128)(2,1)} %bitcast.190) | data formatting | bytes 16777216 | tf_op jit(solution)/shard_map/reshape | solution.py:94
  935.2 91.0 %all-to-all-done.3 = bf16[16,2,512,256]{3,1,0,2:T(2,128)(2,1)} async-done(((bf16[16,2,512,256]{3,1,0,2:T(2,128)(2,1)}), bf16[16,2,512,256]{3,1,0,2:T(2,128)(2,1)}, u32[]{:S(2)}, u32[]{:S(2)}) %all-to-all-start.3) | async-done | bytes 8388640 | tf_op jit(solution)/shard_map/all_to_all | solution.py:144
  1036.5 23.4 %fusion.60 = f32[16,1024,512]{2,1,0:T(8,128)} fusion(bf16[16,512,256]{2,1,0:T(8,128)(2,1)} %fusion.173, bf16[16,512,256]{2,1,0:T(8,128)(2,1)} %get-tuple-element.18, bf16[16,512,256]{2,1,0:T(8,128)(2,1)} %get-tuple-element.17), kind=kOutput, calls=%fused_computation.92 | convolution fusion | flops 8673820672 | bytes 46137344 | tf_op jit(solution)/shard_map/cif,cjf->cij/dot_general | solution.py:84
  1059.9 22.4 %fusion.68 = f32[16,1024,512]{2,1,0:T(8,128)} fusion(bf16[16,512,256]{2,1,0:T(8,128)(2,1)S(1)} %copy-done.2, bf16[16,512,256]{2,1,0:T(8,128)(2,1)} %get-tuple-element.16, bf16[16,512,256]{2,1,0:T(8,128)(2,1)} %get-tuple-element.15), kind=kOutput, calls=%fused_computation.100 | convolution fusion | flops 8673820672 | bytes 46137344 | tf_op jit(solution)/shard_map/cif,cjf->cij/dot_general | solution.py:84
  1082.3 40.6 %add_multiply_fusion = f32[16,1024,512]{2,1,0:T(8,128)} fusion(f32[16,1024,512]{2,1,0:T(8,128)} %fusion.60, f32[16,1024,512]{2,1,0:T(8,128)} %fusion.68, bf16[16,512,256]{2,1,0:T(8,128)(2,1)} %fusion.175, bf16[16,512,256]{2,1,0:T(8,128)(2,1)} %get-tuple-element.14, bf16[16,512,256]{2,1,0:T(8,128)(2,1)} %get-tuple-element.13), kind=kOutput, calls=%fused_computation.1 | convolution fusion | flops 8698986496 | bytes 113246208 | tf_op jit(solution)/shard_map/cif,cjf->cij/dot_general | solution.py:84
  1142.3 19.6 %fusion.112 = bf16[128,256,128]{2,1,0:T(8,128)(2,1)S(1)} fusion(bf16[128,128,256]{2,1,0:T(8,128)(2,1)} %bitcast.185, s32[128]{0:T(128)S(1)} %copy-done.11, s32[128]{0:T(128)S(1)} %copy-done.9, pred[128]{0:T(512)(128)(4,1)S(1)} %copy-done.5, pred[128]{0:T(512)(128)(4,1)S(1)} %copy-done.7), kind=kOutput, calls=%fused_computation.148 | convolution fusion | flops 1078263808 | bytes 16778496 | tf_op jit(solution)/shard_map/oi,ibf->bfo/dot_general | solution.py:149
  1189.4 19.4 %fusion.109 = bf16[128,256,128]{2,1,0:T(8,128)(2,1)S(1)} fusion(bf16[128,128,256]{2,1,0:T(8,128)(2,1)} %bitcast.187, s32[128]{0:T(128)S(1)} %copy-done.11, s32[128]{0:T(128)S(1)} %copy-done.9, pred[128]{0:T(512)(128)(4,1)S(1)} %copy-done.5, pred[128]{0:T(512)(128)(4,1)S(1)} %copy-done.7), kind=kOutput, calls=%fused_computation.147 | convolution fusion | flops 1078263808 | bytes 16778496 | tf_op jit(solution)/shard_map/oi,ibf->bfo/dot_general | solution.py:149
  1245.6 22.7 %fusion.115 = bf16[128,256,128]{2,1,0:T(8,128)(2,1)} fusion(bf16[128,128,256]{2,1,0:T(8,128)(2,1)} %bitcast.183, s32[128]{0:T(128)S(1)} %copy-done.11, s32[128]{0:T(128)S(1)} %copy-done.9, pred[128]{0:T(512)(128)(4,1)S(1)} %copy-done.5, pred[128]{0:T(512)(128)(4,1)S(1)} %copy-done.7), kind=kOutput, calls=%fused_computation.149 | convolution fusion | flops 1078263808 | bytes 16778496 | tf_op jit(solution)/shard_map/oi,ibf->bfo/dot_general | solution.py:149
  1294.9 72.4 %fusion.108 = (bf16[1,128,256,128]{3,2,1,0:T(8,128)(2,1)}, bf16[1,128,256,128]{3,2,1,0:T(8,128)(2,1)}, bf16[1,128,256,128]{3,2,1,0:T(8,128)(2,1)}) fusion(f32[128,1,256,128]{3,2,0,1:T(8,128)} %convert_bitcast_fusion.2, f32[128,1,3,128]{3,2,0,1:T(4,128)S(1)} %convert_element_type.172, f32[128]{0:T(128)S(1)} %copy-done.15, f32[128]{0:T(128)S(1)} %copy-done.16, ...), kind=kLoop, calls=%fused_computation.146 | loop fusion | flops 150994944 | bytes 101255168 | tf_op jit(solution)/shard_map/transpose | solution.py:117
  1367.3 20.7 %pad_maximum_fusion = bf16[3,128,256,128]{3,2,1,0:T(8,128)(2,1)} fusion(bf16[1,128,256,128]{3,2,1,0:T(8,128)(2,1)} %get-tuple-element.27, bf16[1,128,256,128]{3,2,1,0:T(8,128)(2,1)} %get-tuple-element.26, bf16[1,128,256,128]{3,2,1,0:T(8,128)(2,1)} %get-tuple-element.25), kind=kLoop, calls=%fused_computation.5 | loop fusion | flops 25165824 | bytes 50331648 | tf_op jit(solution)/shard_map/concatenate | solution.py:155
  (116 shorter events, 290.7 us)
Async XLA Ops:
  2.0 28.5 %collective-permute-start = (bf16[3,128,3,128]{3,1,2,0:T(8,128)(2,1)S(1)}, bf16[3,128,3,128]{3,1,2,0:T(8,128)(2,1)S(1)}, u32[]{:S(2)}, u32[]{:S(2)}) collective-permute-start(bf16[3,128,3,128]{3,1,2,0:T(8,128)(2,1)S(1)} %copy.73), channel_id=1, source_target_pairs={{0,1},{1,8},{8,9},{9,16},{16,17},{17,24},{24,25},{2,3},{3,10},{10,... | collective-permute-start | bytes 884744 | tf_op jit(solution)/shard_map/ppermute | solution.py:17
  6.9 271.6 %copy-start.4 = (pred[128]{0:T(512)(128)(4,1)}, pred[128]{0:T(512)(128)(4,1)S(1)}, u32[]{:S(2)}) copy-start(pred[128]{0:T(512)(128)(4,1)S(1)} %get-tuple-element.38) | copy-start | bytes 388
  6.9 271.6 %copy-start.6 = (pred[128]{0:T(512)(128)(4,1)}, pred[128]{0:T(512)(128)(4,1)S(1)}, u32[]{:S(2)}) copy-start(pred[128]{0:T(512)(128)(4,1)S(1)} %get-tuple-element.39) | copy-start | bytes 388
  7.0 23.5 %copy-start.18 = (s32[128]{0:T(128)S(1)}, s32[128]{0:T(128)}, u32[]{:S(2)}) copy-start(s32[128]{0:T(128)} %param.6) | copy-start | bytes 1540
  7.0 23.4 %copy-start.12 = (f32[4,64]{1,0:T(4,128)S(1)}, f32[4,64]{1,0:T(4,128)}, u32[]{:S(2)}) copy-start(f32[4,64]{1,0:T(4,128)} %param.8) | copy-start | bytes 3076
  30.5 248.1 %copy-start.8 = (s32[128]{0:T(128)}, s32[128]{0:T(128)S(1)}, u32[]{:S(2)}) copy-start(s32[128]{0:T(128)S(1)} %get-tuple-element.36) | copy-start | bytes 1540
  30.5 248.1 %copy-start.10 = (s32[128]{0:T(128)}, s32[128]{0:T(128)S(1)}, u32[]{:S(2)}) copy-start(s32[128]{0:T(128)S(1)} %get-tuple-element.37) | copy-start | bytes 1540
  83.9 188.7 %all-to-all-start.2 = ((bf16[64,2,128,256]{3,1,2,0:T(2,128)(2,1)}), bf16[64,2,128,256]{3,1,2,0:T(2,128)(2,1)}, u32[]{:S(2)}, u32[]{:S(2)}) async-start(bf16[64,2,128,256]{3,1,2,0:T(2,128)(2,1)} %copy.51), calls=%async_computation.2 | async-start | bytes 16777216 | tf_op jit(solution)/shard_map/all_to_all | solution.py:139
  272.6 188.4 %all-to-all-start.1 = ((bf16[64,2,128,256]{3,1,2,0:T(2,128)(2,1)}), bf16[64,2,128,256]{3,1,2,0:T(2,128)(2,1)}, u32[]{:S(2)}, u32[]{:S(2)}) async-start(bf16[64,2,128,256]{3,1,2,0:T(2,128)(2,1)} %copy.48), calls=%async_computation.1 | async-start | bytes 16777216 | tf_op jit(solution)/shard_map/all_to_all | solution.py:139
  323.5 143.1 %copy-start.3 = (s32[512,512]{1,0:T(8,128)S(1)}, s32[512,512]{1,0:T(8,128)}, u32[]{:S(2)}) copy-start(s32[512,512]{1,0:T(8,128)} %param.7) | copy-start | bytes 3145732
  461.0 188.3 %all-to-all-start = ((bf16[64,2,128,256]{3,1,2,0:T(2,128)(2,1)}), bf16[64,2,128,256]{3,1,2,0:T(2,128)(2,1)}, u32[]{:S(2)}, u32[]{:S(2)}) async-start(bf16[64,2,128,256]{3,1,2,0:T(2,128)(2,1)} %copy.45), calls=%async_computation | async-start | bytes 16777216 | tf_op jit(solution)/shard_map/all_to_all | solution.py:139
  649.3 188.7 %all-to-all-start.4 = ((bf16[16,2,512,256]{3,1,0,2:T(2,128)(2,1)}), bf16[16,2,512,256]{3,1,0,2:T(2,128)(2,1)}, u32[]{:S(2)}, u32[]{:S(2)}) async-start(bf16[16,2,512,256]{3,1,0,2:T(2,128)(2,1)} %copy.60), calls=%async_computation.4 | async-start | bytes 16777216 | tf_op jit(solution)/shard_map/all_to_all | solution.py:144
  685.1 158.5 %copy-start.13 = (f32[4,64]{1,0:T(4,128)S(1)}, f32[4,64]{1,0:T(4,128)}, u32[]{:S(2)}) copy-start(f32[4,64]{1,0:T(4,128)} %param.9) | copy-start | bytes 3076
  838.0 188.3 %all-to-all-start.3 = ((bf16[16,2,512,256]{3,1,0,2:T(2,128)(2,1)}), bf16[16,2,512,256]{3,1,0,2:T(2,128)(2,1)}, u32[]{:S(2)}, u32[]{:S(2)}) async-start(bf16[16,2,512,256]{3,1,0,2:T(2,128)(2,1)} %copy.55), calls=%async_computation.3 | async-start | bytes 16777216 | tf_op jit(solution)/shard_map/all_to_all | solution.py:144
  899.8 21.3 %slice-start.2 = ((s8[8388608]{0:T(1024)(128)(4,1)}), s8[4194304]{0:T(1024)(128)(4,1)S(1)}, s32[]{:S(2)}) async-start(s8[8388608]{0:T(1024)(128)(4,1)} %bitcast.175), calls=%async_computation.8 | async-start | bytes 8388608
  899.8 21.3 %slice-start.3 = ((s8[8388608]{0:T(1024)(128)(4,1)}), s8[4194304]{0:T(1024)(128)(4,1)S(1)}, s32[]{:S(2)}) async-start(s8[8388608]{0:T(1024)(128)(4,1)} %bitcast.175), calls=%async_computation.9 | async-start | bytes 8388608
  899.8 23.5 %slice-start.4 = ((s8[8388608]{0:T(1024)(128)(4,1)}), s8[4194304]{0:T(1024)(128)(4,1)S(1)}, s32[]{:S(2)}) async-start(s8[8388608]{0:T(1024)(128)(4,1)} %bitcast.180), calls=%async_computation.10 | async-start | bytes 8388608
  1026.3 200.1 %all-to-all-start.5 = ((bf16[16,2,512,256]{3,1,0,2:T(2,128)(2,1)}), bf16[16,2,512,256]{3,1,0,2:T(2,128)(2,1)}, u32[]{:S(2)}, u32[]{:S(2)}) async-start(bf16[16,2,512,256]{3,1,0,2:T(2,128)(2,1)} %copy.65), calls=%async_computation.5 | async-start | bytes 16777216 | tf_op jit(solution)/shard_map/all_to_all | solution.py:144
  1036.5 23.4 %copy-start.2 = (bf16[16,512,256]{2,1,0:T(8,128)(2,1)S(1)}, bf16[16,512,256]{2,1,0:T(8,128)(2,1)}, u32[]{:S(2)}) copy-start(bf16[16,512,256]{2,1,0:T(8,128)(2,1)} %fusion.174) | copy-start | bytes 12582916
  1122.9 19.4 %copy-start.5 = (pred[128]{0:T(512)(128)(4,1)S(1)}, pred[128]{0:T(512)(128)(4,1)}, u32[]{:S(2)}) copy-start(pred[128]{0:T(512)(128)(4,1)} %copy-done.4) | copy-start | bytes 388
  1122.9 19.4 %copy-start.7 = (pred[128]{0:T(512)(128)(4,1)S(1)}, pred[128]{0:T(512)(128)(4,1)}, u32[]{:S(2)}) copy-start(pred[128]{0:T(512)(128)(4,1)} %copy-done.6) | copy-start | bytes 388
  1165.3 129.4 %collective-permute-start.2 = (bf16[128,1,3,128]{3,2,0,1:T(4,128)(2,1)S(1)}, bf16[128,1,3,128]{3,2,0,1:T(4,128)(2,1)S(1)}, u32[]{:S(2)}, u32[]{:S(2)}) collective-permute-start(bf16[128,1,3,128]{3,2,0,1:T(4,128)(2,1)S(1)} %slice.216), channel_id=1, source_target_pairs={{0,1},{1,8},{8,9},{9,16},{16,17},{17,24},{24,25},{2,3},{3,10},{10,... | collective-permute-start | bytes 294920 | tf_op jit(solution)/shard_map/ppermute | solution.py:17
  1212.2 82.5 %collective-permute-start.1 = (bf16[128,1,3,128]{3,2,0,1:T(4,128)(2,1)S(1)}, bf16[128,1,3,128]{3,2,0,1:T(4,128)(2,1)S(1)}, u32[]{:S(2)}, u32[]{:S(2)}) collective-permute-start(bf16[128,1,3,128]{3,2,0,1:T(4,128)(2,1)S(1)} %slice.211), channel_id=1, source_target_pairs={{0,1},{1,8},{8,9},{9,16},{16,17},{17,24},{24,25},{2,3},{3,10},{10,... | collective-permute-start | bytes 294920 | tf_op jit(solution)/shard_map/ppermute | solution.py:17
  1280.9 13.9 collective-permute-start.3
  (11 other events, 124.5 us)
where the time goes:
time: 1400 us; the launch traced here: 1390 us
  waiting for transfers between devices  552 us (39%)
  matrix products  308 us (22%)
  local copies, waits for them, and re-layouts  245 us (18%)
  other arithmetic  233 us (17%)
  starting transfers between devices  49 us (4%)
    all_to_all x3, waiting for transfers between devices, per_device(): lax.all_to_all(spectra_list[batch_step], 'chan', split_axis=0, concat_axi...  325 us
    all_to_all x3, waiting for transfers between devices, per_device(): lax.all_to_all(form_beams(turned, steering_matrix), 'chan', split_axis=2,...  227 us
    dot_general x3, matrix products, channelize(): jnp.einsum('oi,afi->oaf', forward, weighted, preferred_element_type=jnp.f...  96.2 us
    dot_general x3, matrix products, gram_block(): jnp.einsum('cif,cjf->cij', stacked, left_part, preferred_element_type=jnp...  86.4 us
    transpose x1, other arithmetic, synthesize(): return jnp.transpose(weighted.astype(jnp.bfloat16), (1, 0, 2, 3))  72.4 us
    another operation x1, other arithmetic  70 us
    dot_general x3, matrix products, form_beams(): jnp.einsum('goq,gqk->gok', steering_matrix, flattened_rows, preferred_ele...  63.9 us
    reshape x6, local copies, waits for them, and re-layouts, channelize(): spectra.astype(jnp.bfloat16)  63.7 us
  transfers between devices with their start and end apart: 10, of which 5 were waited for; matrix products, arithmetic and copies ran while one was open for 45% of the time, Pallas kernels for 0%

commit v1 on v0

--- a/solution.py
+++ b/solution.py
@@ -136,9 +136,20 @@
     gram_total = None
     beam_list = []
     for batch_step in range(MB):
-        turned = lax.all_to_all(
-            spectra_list[batch_step], "chan", split_axis=0, concat_axis=2, tiled=True
-        )
+        ways, here = (lax.axis_size("chan"), lax.axis_index("chan"))
+        width = spectra_list[batch_step].shape[0] // ways
+        lengths = list(spectra_list[batch_step].shape)
+        lengths[0] = width
+        height = lengths[2]
+        lengths[2] = height * ways
+        turned = jnp.zeros(lengths, spectra_list[batch_step].dtype)
+        for mask in range(ways):
+            part = lax.dynamic_slice_in_dim(
+                spectra_list[batch_step], (here ^ mask) * width, width, axis=0
+            )
+            if mask:
+                part = lax.ppermute(part, "chan", [(d, d ^ mask) for d in range(ways)])
+            turned = lax.dynamic_update_slice_in_dim(turned, part, (here ^ mask) * height, axis=2)
         gram_piece = gram_block(turned)
         gram_total = gram_piece if batch_step == 0 else gram_total + gram_piece
         piece = lax.all_to_all(

time: 1400 us -> 1550 us (1.11)
  starting transfers between devices: 49 us -> 168 us
  local copies, waits for them, and re-layouts: 245 us -> 279 us
    ppermute x0 -> x9, waiting for transfers between devices: none -> 546 us  [per_device(): part = lax.ppermute(part, 'chan', [(d, d ^ mask) for d in range(ways)])]
    all_to_all x3 -> x0, waiting for transfers between devices: 325 us -> none  [per_device(): lax.all_to_all(spectra_list[batch_step], 'chan', split_axis=0, concat_axi...]
    all_to_all x3, waiting for transfers between devices: 227 us -> 0.01 us  [per_device(): lax.all_to_all(form_beams(turned, steering_matrix), 'chan', split_axis=2,...]
    all_to_all x3, starting transfers between devices: 17.5 us -> 137 us  [per_device(): lax.all_to_all(form_beams(turned, steering_matrix), 'chan', split_axis=2,...]
    all_to_all x6 -> x0, local copies, waits for them, and re-layouts: 51.1 us -> none  [per_device(): lax.all_to_all(spectra_list[batch_step], 'chan', split_axis=0, concat_axi...]
    dynamic_update_slice x0 -> x15, local copies, waits for them, and re-layouts: none -> 48.3 us  [per_device(): lax.dynamic_update_slice_in_dim(turned, part, (here ^ mask) * height, axi...]
    dynamic_slice x0 -> x3, local copies, waits for them, and re-layouts: none -> 28.3 us  [per_device(): lax.dynamic_slice_in_dim(spectra_list[batch_step], (here ^ mask) * width,...]
    reshape x6 -> x3, local copies, waits for them, and re-layouts: 63.7 us -> 39.3 us  [channelize(): spectra.astype(jnp.bfloat16)]
  transfers between devices with their start and end apart: 10 -> 16, of which waited for: 5 -> 6; matrix products, arithmetic and copies ran while one was open for 45% -> 40% of each run, Pallas kernels for 0% -> 0%
where the time goes in v1:
time: 1550 us; the launch traced here: 1540 us
  waiting for transfers between devices  546 us (35%)
  matrix products  309 us (20%)
  local copies, waits for them, and re-layouts  279 us (18%)
  other arithmetic  239 us (15%)
  starting transfers between devices  168 us (11%)
    ppermute x9, waiting for transfers between devices, per_device(): part = lax.ppermute(part, 'chan', [(d, d ^ mask) for d in range(ways)])  546 us
    all_to_all x3, starting transfers between devices, per_device(): lax.all_to_all(form_beams(turned, steering_matrix), 'chan', split_axis=2,...  137 us
    dot_general x3, matrix products, channelize(): jnp.einsum('oi,afi->oaf', forward, weighted, preferred_element_type=jnp.f...  96.3 us
    dot_general x3, matrix products, gram_block(): jnp.einsum('cif,cjf->cij', stacked, left_part, preferred_element_type=jnp...  86.9 us
    transpose x1, other arithmetic, synthesize(): return jnp.transpose(weighted.astype(jnp.bfloat16), (1, 0, 2, 3))  74.3 us
    another operation x1, other arithmetic  70.5 us
    dot_general x3, matrix products, form_beams(): jnp.einsum('goq,gqk->gok', steering_matrix, flattened_rows, preferred_ele...  64.4 us
    dot_general x3, matrix products, per_device(): jnp.einsum('oi,ibf->bfo', inverse_result, flattened_rows, preferred_eleme...  61.6 us
  transfers between devices with their start and end apart: 16, of which 6 were waited for; matrix products, arithmetic and copies ran while one was open for 40% of the time, Pallas kernels for 0%

profile of v1, /device:TPU:0, one launch (start us, length us, event | category | flops | bytes accessed | tf_op | source)
XLA Modules:
  0.0 1542.3 jit_solution(742002470681222398)
XLA Ops:
  7.0 23.8 %bitcast_convert_fusion = (f32[128,256,128]{2,1,0:T(8,128)}, f32[128,256,128]{2,1,0:T(8,128)}, f32[128,256,128]{2,1,0:T(8,128)}) fusion(bf16[3,128,256,128]{3,2,1,0:T(8,128)(2,1)} %param.5), kind=kLoop, calls=%fused_computation.133 | loop fusion | flops 12582912 | bytes 75497472 | tf_op jit(solution)/shard_map/convert_element_type | solution.py:66
  32.1 32.5 %multiply_convert_fusion.4 = bf16[128,128,256]{2,0,1:T(8,128)(2,1)} fusion(f32[128]{0:T(128)S(1)} %convert_element_type.152, f32[128,3,128]{2,1,0:T(4,128)S(1)} %copy.73, f32[128,256,128]{2,1,0:T(8,128)} %get-tuple-element.12, f32[128]{0:T(128)S(1)} %get-tuple-element.45, f32[128]{0:T(128)S(1)} %get-tuple-element.46, f32[128]{0:T(128)S(1)} %get-tuple-element.47, ...), kind=kOutput, calls=%fused_computation.122 | convolution fusion | flops 1128595456 | bytes 25366272 | tf_op jit(solution)/shard_map/oi,afi->oaf/dot_general | solution.py:75
  99.2 70.5 %fusion.102 = (bf16[16,512,512]{2,1,0:T(8,128)(2,1)}, bf16[16,512,512]{2,1,0:T(8,128)(2,1)}, bf16[16,512,512]{2,1,0:T(8,128)(2,1)}) fusion(s32[512,512]{1,0:T(8,128)S(1)} %copy.83, s32[16]{0:T(128)S(1)} %copy-done.18), kind=kLoop, calls=%fused_computation.143 | loop fusion | flops 75497472 | bytes 26214464 | tf_op jit(solution)/shard_map/convert.11
  189.4 46.5 %collective-permute-done.5 = bf16[16,2,128,256]{3,2,0,1:T(8,128)(2,1)} collective-permute-done((bf16[16,2,128,256]{3,2,0,1:T(8,128)(2,1)}, bf16[16,2,128,256]{3,2,0,1:T(8,128)(2,1)}, u32[]{:S(2)}, u32[]{:S(2)}) %collective-permute-start.5) | collective-permute-done | bytes 2097184 | tf_op jit(solution)/shard_map/ppermute | solution.py:151
  249.8 21.2 %multiply_convert_fusion.1 = bf16[16,1024,256]{2,1,0:T(8,128)(2,1)} fusion(bf16[16,1024,256]{2,1,0:T(8,128)(2,1)} %bitcast.161, bf16[16,512,512]{2,1,0:T(8,128)(2,1)} %get-tuple-element.33, bf16[16,512,512]{2,1,0:T(8,128)(2,1)} %get-tuple-element.32, bf16[16,512,512]{2,1,0:T(8,128)(2,1)} %get-tuple-element.31), kind=kOutput, calls=%fused_computation.117 | convolution fusion | flops 8732540928 | bytes 41943040 | tf_op jit(solution)/shard_map/goq,gqk->gok/dot_general | solution.py:90
  287.4 43.3 %all-to-all-start.1 = ((bf16[16,2,512,256]{3,1,0,2:T(2,128)(2,1)}), bf16[16,2,512,256]{3,1,0,2:T(2,128)(2,1)}, u32[]{:S(2)}, u32[]{:S(2)}) async-start(bf16[16,2,512,256]{3,1,0,2:T(2,128)(2,1)} %copy.90), calls=%async_computation.1 | async-start | bytes 16777216 | tf_op jit(solution)/shard_map/all_to_all | solution.py:155
  330.9 31.9 %multiply_convert_fusion.5 = bf16[128,128,256]{2,0,1:T(8,128)(2,1)} fusion(f32[128]{0:T(128)S(1)} %copy-done.29, f32[128,3,128]{2,1,0:T(4,128)S(1)} %copy.68, f32[128,256,128]{2,1,0:T(8,128)} %get-tuple-element.11, f32[128]{0:T(128)S(1)} %copy-done.22, f32[128]{0:T(128)S(1)} %copy-done.24, f32[128]{0:T(128)S(1)} %copy-done.26, f32[128]{0:T(128)S(1)} %copy-done.20, ...), kind=kOutput, calls=%fused_computation.123 | convolution fusion | flops 1128595456 | bytes 25366272 | tf_op jit(solution)/shard_map/oi,afi->oaf/dot_general | solution.py:75
  401.8 110.0 %collective-permute-done.1 = bf16[16,2,128,256]{3,2,0,1:T(8,128)(2,1)S(1)} collective-permute-done((bf16[16,2,128,256]{3,2,0,1:T(8,128)(2,1)S(1)}, bf16[16,2,128,256]{3,2,0,1:T(8,128)(2,1)S(1)}, u32[]{:S(2)}, u32[]{:S(2)}) %collective-permute-start.1) | collective-permute-done | bytes 2097184 | tf_op jit(solution)/shard_map/ppermute | solution.py:151
  513.2 134.9 %collective-permute-done.2 = bf16[16,2,128,256]{3,2,0,1:T(8,128)(2,1)S(1)} collective-permute-done((bf16[16,2,128,256]{3,2,0,1:T(8,128)(2,1)S(1)}, bf16[16,2,128,256]{3,2,0,1:T(8,128)(2,1)S(1)}, u32[]{:S(2)}, u32[]{:S(2)}) %collective-permute-start.2) | collective-permute-done | bytes 2097184 | tf_op jit(solution)/shard_map/ppermute | solution.py:151
  658.5 21.8 %multiply_convert_fusion.2 = bf16[16,1024,256]{2,1,0:T(8,128)(2,1)} fusion(bf16[16,1024,256]{2,1,0:T(8,128)(2,1)} %bitcast.164, bf16[16,512,512]{2,1,0:T(8,128)(2,1)} %get-tuple-element.33, bf16[16,512,512]{2,1,0:T(8,128)(2,1)} %get-tuple-element.32, bf16[16,512,512]{2,1,0:T(8,128)(2,1)} %get-tuple-element.31), kind=kOutput, calls=%fused_computation.118 | convolution fusion | flops 8732540928 | bytes 41943040 | tf_op jit(solution)/shard_map/goq,gqk->gok/dot_general | solution.py:90
  696.8 46.2 %all-to-all-start = ((bf16[16,2,512,256]{3,1,0,2:T(2,128)(2,1)}), bf16[16,2,512,256]{3,1,0,2:T(2,128)(2,1)}, u32[]{:S(2)}, u32[]{:S(2)}) async-start(bf16[16,2,512,256]{3,1,0,2:T(2,128)(2,1)} %copy.85), calls=%async_computation | async-start | bytes 16777216 | tf_op jit(solution)/shard_map/all_to_all | solution.py:155
  743.0 32.0 %multiply_convert_fusion.3 = bf16[128,128,256]{2,0,1:T(8,128)(2,1)} fusion(f32[128]{0:T(128)S(1)} %copy-done.29, f32[128,3,128]{2,1,0:T(4,128)S(1)} %copy.78, f32[128,256,128]{2,1,0:T(8,128)} %get-tuple-element.10, f32[128]{0:T(128)S(1)} %copy-done.22, f32[128]{0:T(128)S(1)} %copy-done.24, f32[128]{0:T(128)S(1)} %copy-done.26, f32[128]{0:T(128)S(1)} %copy-done.20, ...), kind=kOutput, calls=%fused_computation.121 | convolution fusion | flops 1128595456 | bytes 25366272 | tf_op jit(solution)/shard_map/oi,afi->oaf/dot_general | solution.py:75
  814.6 109.5 %collective-permute-done.7 = bf16[16,2,128,256]{3,2,0,1:T(8,128)(2,1)S(1)} collective-permute-done((bf16[16,2,128,256]{3,2,0,1:T(8,128)(2,1)S(1)}, bf16[16,2,128,256]{3,2,0,1:T(8,128)(2,1)S(1)}, u32[]{:S(2)}, u32[]{:S(2)}) %collective-permute-start.7) | collective-permute-done | bytes 2097184 | tf_op jit(solution)/shard_map/ppermute | solution.py:151
  925.5 135.6 %collective-permute-done.8 = bf16[16,2,128,256]{3,2,0,1:T(8,128)(2,1)S(1)} collective-permute-done((bf16[16,2,128,256]{3,2,0,1:T(8,128)(2,1)S(1)}, bf16[16,2,128,256]{3,2,0,1:T(8,128)(2,1)S(1)}, u32[]{:S(2)}, u32[]{:S(2)}) %collective-permute-start.8) | collective-permute-done | bytes 2097184 | tf_op jit(solution)/shard_map/ppermute | solution.py:151
  1071.5 21.4 %multiply_convert_fusion = bf16[16,1024,256]{2,1,0:T(8,128)(2,1)} fusion(bf16[16,1024,256]{2,1,0:T(8,128)(2,1)} %bitcast.160, bf16[16,512,512]{2,1,0:T(8,128)(2,1)} %get-tuple-element.33, bf16[16,512,512]{2,1,0:T(8,128)(2,1)} %get-tuple-element.32, bf16[16,512,512]{2,1,0:T(8,128)(2,1)} %get-tuple-element.31), kind=kOutput, calls=%fused_computation.116 | convolution fusion | flops 8732540928 | bytes 41943040 | tf_op jit(solution)/shard_map/goq,gqk->gok/dot_general | solution.py:90
  1136.0 47.2 %all-to-all-start.2 = ((bf16[16,2,512,256]{3,1,0,2:T(2,128)(2,1)}), bf16[16,2,512,256]{3,1,0,2:T(2,128)(2,1)}, u32[]{:S(2)}, u32[]{:S(2)}) async-start(bf16[16,2,512,256]{3,1,0,2:T(2,128)(2,1)} %copy.95), calls=%async_computation.2 | async-start | bytes 16777216 | tf_op jit(solution)/shard_map/all_to_all | solution.py:155
  1187.7 23.4 %fusion.60 = f32[16,1024,512]{2,1,0:T(8,128)} fusion(bf16[16,512,256]{2,1,0:T(8,128)(2,1)} %fusion.173, bf16[16,512,256]{2,1,0:T(8,128)(2,1)} %get-tuple-element.26, bf16[16,512,256]{2,1,0:T(8,128)(2,1)} %get-tuple-element.25), kind=kOutput, calls=%fused_computation.92 | convolution fusion | flops 8673820672 | bytes 46137344 | tf_op jit(solution)/shard_map/cif,cjf->cij/dot_general | solution.py:84
  1211.1 22.7 %fusion.68 = f32[16,1024,512]{2,1,0:T(8,128)} fusion(bf16[16,512,256]{2,1,0:T(8,128)(2,1)S(1)} %copy-done.2, bf16[16,512,256]{2,1,0:T(8,128)(2,1)} %get-tuple-element.20, bf16[16,512,256]{2,1,0:T(8,128)(2,1)} %get-tuple-element.19), kind=kOutput, calls=%fused_computation.100 | convolution fusion | flops 8673820672 | bytes 46137344 | tf_op jit(solution)/shard_map/cif,cjf->cij/dot_general | solution.py:84
  1233.8 40.8 %add_multiply_fusion = f32[16,1024,512]{2,1,0:T(8,128)} fusion(f32[16,1024,512]{2,1,0:T(8,128)} %fusion.60, f32[16,1024,512]{2,1,0:T(8,128)} %fusion.68, bf16[16,512,256]{2,1,0:T(8,128)(2,1)} %fusion.175, bf16[16,512,256]{2,1,0:T(8,128)(2,1)} %get-tuple-element.14, bf16[16,512,256]{2,1,0:T(8,128)(2,1)} %get-tuple-element.13), kind=kOutput, calls=%fused_computation.1 | convolution fusion | flops 8698986496 | bytes 113246208 | tf_op jit(solution)/shard_map/cif,cjf->cij/dot_general | solution.py:84
  1294.0 19.6 %fusion.112 = bf16[128,256,128]{2,1,0:T(8,128)(2,1)S(1)} fusion(bf16[128,128,256]{2,1,0:T(8,128)(2,1)} %bitcast.155, s32[128]{0:T(128)S(1)} %copy-done.11, s32[128]{0:T(128)S(1)} %copy-done.9, pred[128]{0:T(512)(128)(4,1)S(1)} %copy-done.5, pred[128]{0:T(512)(128)(4,1)S(1)} %copy-done.7), kind=kOutput, calls=%fused_computation.148 | convolution fusion | flops 1078263808 | bytes 16778496 | tf_op jit(solution)/shard_map/oi,ibf->bfo/dot_general | solution.py:160
  1341.5 19.4 %fusion.109 = bf16[128,256,128]{2,1,0:T(8,128)(2,1)S(1)} fusion(bf16[128,128,256]{2,1,0:T(8,128)(2,1)} %bitcast.157, s32[128]{0:T(128)S(1)} %copy-done.11, s32[128]{0:T(128)S(1)} %copy-done.9, pred[128]{0:T(512)(128)(4,1)S(1)} %copy-done.5, pred[128]{0:T(512)(128)(4,1)S(1)} %copy-done.7), kind=kOutput, calls=%fused_computation.147 | convolution fusion | flops 1078263808 | bytes 16778496 | tf_op jit(solution)/shard_map/oi,ibf->bfo/dot_general | solution.py:160
  1397.6 22.6 %fusion.115 = bf16[128,256,128]{2,1,0:T(8,128)(2,1)} fusion(bf16[128,128,256]{2,1,0:T(8,128)(2,1)} %bitcast.153, s32[128]{0:T(128)S(1)} %copy-done.11, s32[128]{0:T(128)S(1)} %copy-done.9, pred[128]{0:T(512)(128)(4,1)S(1)} %copy-done.5, pred[128]{0:T(512)(128)(4,1)S(1)} %copy-done.7), kind=kOutput, calls=%fused_computation.149 | convolution fusion | flops 1078263808 | bytes 16778496 | tf_op jit(solution)/shard_map/oi,ibf->bfo/dot_general | solution.py:160
  1447.0 74.3 %fusion.108 = (bf16[1,128,256,128]{3,2,1,0:T(8,128)(2,1)}, bf16[1,128,256,128]{3,2,1,0:T(8,128)(2,1)}, bf16[1,128,256,128]{3,2,1,0:T(8,128)(2,1)}) fusion(f32[128,1,256,128]{3,2,0,1:T(8,128)} %convert_bitcast_fusion.2, f32[128,1,3,128]{3,2,0,1:T(4,128)S(1)} %convert_element_type.172, f32[128]{0:T(128)S(1)} %copy-done.15, f32[128]{0:T(128)S(1)} %copy-done.16, ...), kind=kLoop, calls=%fused_computation.146 | loop fusion | flops 150994944 | bytes 101255168 | tf_op jit(solution)/shard_map/transpose | solution.py:117
  1521.3 20.7 %pad_maximum_fusion = bf16[3,128,256,128]{3,2,1,0:T(8,128)(2,1)} fusion(bf16[1,128,256,128]{3,2,1,0:T(8,128)(2,1)} %get-tuple-element.39, bf16[1,128,256,128]{3,2,1,0:T(8,128)(2,1)} %get-tuple-element.38, bf16[1,128,256,128]{3,2,1,0:T(8,128)(2,1)} %get-tuple-element.37), kind=kLoop, calls=%fused_computation.5 | loop fusion | flops 25165824 | bytes 50331648 | tf_op jit(solution)/shard_map/concatenate | solution.py:166
  (156 shorter events, 369.3 us)
Async XLA Ops:
  2.0 29.9 %collective-permute-start = (bf16[3,128,3,128]{3,1,2,0:T(8,128)(2,1)S(1)}, bf16[3,128,3,128]{3,1,2,0:T(8,128)(2,1)S(1)}, u32[]{:S(2)}, u32[]{:S(2)}) collective-permute-start(bf16[3,128,3,128]{3,1,2,0:T(8,128)(2,1)S(1)} %copy.100), channel_id=1, source_target_pairs={{0,1},{1,8},{8,9},{9,16},{16,17},{17,24},{24,25},{2,3},{3,10},{10,... | collective-permute-start | bytes 884744 | tf_op jit(solution)/shard_map/ppermute | solution.py:17
  7.0 736.0 %copy-start.4 = (pred[128]{0:T(512)(128)(4,1)}, pred[128]{0:T(512)(128)(4,1)S(1)}, u32[]{:S(2)}) copy-start(pred[128]{0:T(512)(128)(4,1)S(1)} %get-tuple-element.50) | copy-start | bytes 388
  7.0 736.0 %copy-start.6 = (pred[128]{0:T(512)(128)(4,1)}, pred[128]{0:T(512)(128)(4,1)S(1)}, u32[]{:S(2)}) copy-start(pred[128]{0:T(512)(128)(4,1)S(1)} %get-tuple-element.51) | copy-start | bytes 388
  7.0 736.0 %copy-start.8 = (s32[128]{0:T(128)}, s32[128]{0:T(128)S(1)}, u32[]{:S(2)}) copy-start(s32[128]{0:T(128)S(1)} %get-tuple-element.48) | copy-start | bytes 1540
  7.0 736.0 %copy-start.10 = (s32[128]{0:T(128)}, s32[128]{0:T(128)S(1)}, u32[]{:S(2)}) copy-start(s32[128]{0:T(128)S(1)} %get-tuple-element.49) | copy-start | bytes 1540
  94.8 91.4 %collective-permute-start.4 = (bf16[16,2,128,256]{3,2,0,1:T(8,128)(2,1)}, bf16[16,2,128,256]{3,2,0,1:T(8,128)(2,1)}, u32[]{:S(2)}, u32[]{:S(2)}) collective-permute-start(bf16[16,2,128,256]{3,2,0,1:T(8,128)(2,1)} %copy.106), channel_id=1, source_target_pairs={{0,2},{2,0},{4,6},{6,4},{1,3},{3,1},{5,7},{7,5},{8,10},{10,8},{12,... | collective-permute-start | bytes 6291464 | tf_op jit(solution)/shard_map/ppermute | solution.py:151
  96.4 139.6 %collective-permute-start.5 = (bf16[16,2,128,256]{3,2,0,1:T(8,128)(2,1)}, bf16[16,2,128,256]{3,2,0,1:T(8,128)(2,1)}, u32[]{:S(2)}, u32[]{:S(2)}) collective-permute-start(bf16[16,2,128,256]{3,2,0,1:T(8,128)(2,1)} %copy.107), channel_id=1, source_target_pairs={{0,4},{2,6},{4,0},{6,2},{1,5},{3,7},{5,1},{7,3},{8,12},{10,14},{12... | collective-permute-start | bytes 6291464 | tf_op jit(solution)/shard_map/ppermute | solution.py:151
  98.9 140.2 %collective-permute-start.6 = (bf16[16,2,128,256]{3,2,0,1:T(8,128)(2,1)}, bf16[16,2,128,256]{3,2,0,1:T(8,128)(2,1)}, u32[]{:S(2)}, u32[]{:S(2)}) collective-permute-start(bf16[16,2,128,256]{3,2,0,1:T(8,128)(2,1)} %copy.108), channel_id=1, source_target_pairs={{0,6},{2,4},{4,2},{6,0},{1,7},{3,5},{5,3},{7,1},{8,14},{10,12},{12... | collective-permute-start | bytes 6291464 | tf_op jit(solution)/shard_map/ppermute | solution.py:151
  271.0 59.9 %copy-start.22 = (f32[128]{0:T(128)S(1)}, f32[128]{0:T(128)}, u32[]{:S(2)}) copy-start(f32[128]{0:T(128)} %copy-done.21) | copy-start | bytes 1540
  271.0 59.9 %copy-start.24 = (f32[128]{0:T(128)S(1)}, f32[128]{0:T(128)}, u32[]{:S(2)}) copy-start(f32[128]{0:T(128)} %copy-done.23) | copy-start | bytes 1540
  271.0 59.9 %copy-start.26 = (f32[128]{0:T(128)S(1)}, f32[128]{0:T(128)}, u32[]{:S(2)}) copy-start(f32[128]{0:T(128)} %copy-done.25) | copy-start | bytes 1540
  271.0 59.9 %copy-start.29 = (f32[128]{0:T(128)S(1)}, f32[128]{0:T(128)}, u32[]{:S(2)}) copy-start(f32[128]{0:T(128)} %copy-done.28) | copy-start | bytes 1540
  287.4 409.3 %all-to-all-start.1 = ((bf16[16,2,512,256]{3,1,0,2:T(2,128)(2,1)}), bf16[16,2,512,256]{3,1,0,2:T(2,128)(2,1)}, u32[]{:S(2)}, u32[]{:S(2)}) async-start(bf16[16,2,512,256]{3,1,0,2:T(2,128)(2,1)} %copy.90), calls=%async_computation.1 | async-start | bytes 16777216 | tf_op jit(solution)/shard_map/all_to_all | solution.py:155
  386.4 125.3 %collective-permute-start.1 = (bf16[16,2,128,256]{3,2,0,1:T(8,128)(2,1)S(1)}, bf16[16,2,128,256]{3,2,0,1:T(8,128)(2,1)S(1)}, u32[]{:S(2)}, u32[]{:S(2)}) collective-permute-start(bf16[16,2,128,256]{3,2,0,1:T(8,128)(2,1)S(1)} %copy.102), channel_id=1, source_target_pairs={{0,2},{2,0},{4,6},{6,4},{1,3},{3,1},{5,7},{7,5},{8,10},{10,8},{12,... | collective-permute-start | bytes 6291464 | tf_op jit(solution)/shard_map/ppermute | solution.py:151
  391.0 257.2 %collective-permute-start.2 = (bf16[16,2,128,256]{3,2,0,1:T(8,128)(2,1)S(1)}, bf16[16,2,128,256]{3,2,0,1:T(8,128)(2,1)S(1)}, u32[]{:S(2)}, u32[]{:S(2)}) collective-permute-start(bf16[16,2,128,256]{3,2,0,1:T(8,128)(2,1)S(1)} %copy.103), channel_id=1, source_target_pairs={{0,4},{2,6},{4,0},{6,2},{1,5},{3,7},{5,1},{7,3},{8,12},{10,14},{12... | collective-permute-start | bytes 6291464 | tf_op jit(solution)/shard_map/ppermute | solution.py:151
  393.3 256.3 %collective-permute-start.3 = (bf16[16,2,128,256]{3,2,0,1:T(8,128)(2,1)S(1)}, bf16[16,2,128,256]{3,2,0,1:T(8,128)(2,1)S(1)}, u32[]{:S(2)}, u32[]{:S(2)}) collective-permute-start(bf16[16,2,128,256]{3,2,0,1:T(8,128)(2,1)S(1)} %copy.104), channel_id=1, source_target_pairs={{0,6},{2,4},{4,2},{6,0},{1,7},{3,5},{5,3},{7,1},{8,14},{10,12},{12... | collective-permute-start | bytes 6291464 | tf_op jit(solution)/shard_map/ppermute | solution.py:151
  696.8 439.3 %all-to-all-start = ((bf16[16,2,512,256]{3,1,0,2:T(2,128)(2,1)}), bf16[16,2,512,256]{3,1,0,2:T(2,128)(2,1)}, u32[]{:S(2)}, u32[]{:S(2)}) async-start(bf16[16,2,512,256]{3,1,0,2:T(2,128)(2,1)} %copy.85), calls=%async_computation | async-start | bytes 16777216 | tf_op jit(solution)/shard_map/all_to_all | solution.py:155
  798.6 125.4 %collective-permute-start.7 = (bf16[16,2,128,256]{3,2,0,1:T(8,128)(2,1)S(1)}, bf16[16,2,128,256]{3,2,0,1:T(8,128)(2,1)S(1)}, u32[]{:S(2)}, u32[]{:S(2)}) collective-permute-start(bf16[16,2,128,256]{3,2,0,1:T(8,128)(2,1)S(1)} %copy.110), channel_id=1, source_target_pairs={{0,2},{2,0},{4,6},{6,4},{1,3},{3,1},{5,7},{7,5},{8,10},{10,8},{12,... | collective-permute-start | bytes 6291464 | tf_op jit(solution)/shard_map/ppermute | solution.py:151
  803.3 257.7 %collective-permute-start.8 = (bf16[16,2,128,256]{3,2,0,1:T(8,128)(2,1)S(1)}, bf16[16,2,128,256]{3,2,0,1:T(8,128)(2,1)S(1)}, u32[]{:S(2)}, u32[]{:S(2)}) collective-permute-start(bf16[16,2,128,256]{3,2,0,1:T(8,128)(2,1)S(1)} %copy.111), channel_id=1, source_target_pairs={{0,4},{2,6},{4,0},{6,2},{1,5},{3,7},{5,1},{7,3},{8,12},{10,14},{12... | collective-permute-start | bytes 6291464 | tf_op jit(solution)/shard_map/ppermute | solution.py:151
  805.5 257.0 %collective-permute-start.9 = (bf16[16,2,128,256]{3,2,0,1:T(8,128)(2,1)S(1)}, bf16[16,2,128,256]{3,2,0,1:T(8,128)(2,1)S(1)}, u32[]{:S(2)}, u32[]{:S(2)}) collective-permute-start(bf16[16,2,128,256]{3,2,0,1:T(8,128)(2,1)S(1)} %copy.112), channel_id=1, source_target_pairs={{0,6},{2,4},{4,2},{6,0},{1,7},{3,5},{5,3},{7,1},{8,14},{10,12},{12... | collective-permute-start | bytes 6291464 | tf_op jit(solution)/shard_map/ppermute | solution.py:151
  1136.0 242.4 %all-to-all-start.2 = ((bf16[16,2,512,256]{3,1,0,2:T(2,128)(2,1)}), bf16[16,2,512,256]{3,1,0,2:T(2,128)(2,1)}, u32[]{:S(2)}, u32[]{:S(2)}) async-start(bf16[16,2,512,256]{3,1,0,2:T(2,128)(2,1)} %copy.95), calls=%async_computation.2 | async-start | bytes 16777216 | tf_op jit(solution)/shard_map/all_to_all | solution.py:155
  1316.9 129.9 %collective-permute-start.11 = (bf16[128,1,3,128]{3,2,0,1:T(4,128)(2,1)S(1)}, bf16[128,1,3,128]{3,2,0,1:T(4,128)(2,1)S(1)}, u32[]{:S(2)}, u32[]{:S(2)}) collective-permute-start(bf16[128,1,3,128]{3,2,0,1:T(4,128)(2,1)S(1)} %slice.216), channel_id=1, source_target_pairs={{0,1},{1,8},{8,9},{9,16},{16,17},{17,24},{24,25},{2,3},{3,10},{10,... | collective-permute-start | bytes 294920 | tf_op jit(solution)/shard_map/ppermute | solution.py:17
  1364.3 82.6 %collective-permute-start.10 = (bf16[128,1,3,128]{3,2,0,1:T(4,128)(2,1)S(1)}, bf16[128,1,3,128]{3,2,0,1:T(4,128)(2,1)S(1)}, u32[]{:S(2)}, u32[]{:S(2)}) collective-permute-start(bf16[128,1,3,128]{3,2,0,1:T(4,128)(2,1)S(1)} %slice.211), channel_id=1, source_target_pairs={{0,1},{1,8},{8,9},{9,16},{16,17},{17,24},{24,25},{2,3},{3,10},{10,... | collective-permute-start | bytes 294920 | tf_op jit(solution)/shard_map/ppermute | solution.py:17
  1432.9 14.0 collective-permute-start.12
  (22 other events, 504.3 us)
